TPU v7x, 128 devices: a whole 4x4x4 slice. The times are simulated.
128 devices in a mesh: ckpt: 4 (over z_hi, core), space: 32 (over y, x, z_lo).
Axes of the slice: x: 4, y: 4, z: 4 (z_hi: 2, z_lo: 2; z = z_hi * 2 + z_lo), core: 2. Of those that a mesh axis runs over, the one named last changes fastest.
Arguments:
- checkpoint: float32 [32, 6, 16, 16, 128], P('space', None, 'ckpt'), may hold values from -5 to 5
- seeds: float32 [4, 32, 6, 16, 16, 128], P('ckpt', 'space'), may hold values from -6 to 6
- cell_rate: float32 [32, 16, 16, 128], P('space'), may hold values from 0.5 to 2
- flux_mats: float32 [3, 6, 6], replicated, may hold values from -1.25 to 1.25
- owner: int32 [32], replicated, may hold values from 0 to 31, each once
- neighbours: int32 [32, 6], replicated, may hold values from 0 to 31, as said below
- orientation: int32 [32, 6], replicated, may hold values from 0 to 3, as said below
Outputs:
- adjoint: float32 [4, 32, 6, 16, 16, 128], P('ckpt', 'space')
- final_state: float32 [32, 6, 16, 16, 128], P('space')
Inputs may be any that keep to these rules, and one draw needn't show every extreme that they name: owner lists each space index once. The block across the -x face of neighbours[b, 0] is b, across the +x face of neighbours[b, 1] is b, and likewise for y and z; a block may be its own neighbour. orientation[b, f] equals the code of the same face seen from the block across it.
All inputs are finite; a program needn't handle non-finite values.
Results may differ from a plain program's by a relative error of at most 0.0001.
Values sent between devices are 32-bit elements; how exact they have to be, the bound alone decides.
A program may use at most 128 MiB of HBM per device.

v0:
```python
import jax
import jax.numpy as jnp
from jax import lax
from jax.sharding import PartitionSpec as P

STEPS = 2
time_step = 0.05
damping = 0.015


def boundary(field, side):
    layer_axis = field.ndim - 3 + side // 2
    location = field.shape[layer_axis] - 1 if side % 2 == 0 else 0
    return lax.index_in_dim(field, location, layer_axis, keepdims=False)


def reorient(face, flips):
    face = jnp.where(flips % 2 == 1, jnp.flip(face, -2), face)
    return jnp.where(flips // 2 % 2 == 1, jnp.flip(face, -1), face)


def pad_with(field, ghosts):
    padded = jnp.pad(field, [(0, 0)] + [(1, 1)] * 3)
    for side in range(6):
        layer_axis = side // 2
        location = padded.shape[layer_axis + 1] - 1 if side % 2 == 0 else 0
        if layer_axis == 0:
            padded = padded.at[:, location, 1:-1, 1:-1].set(ghosts[side])
        elif layer_axis == 1:
            padded = padded.at[:, 1:-1, location, 1:-1].set(ghosts[side])
        else:
            padded = padded.at[:, 1:-1, 1:-1, location].set(ghosts[side])
    return padded


def ghost_layer(padded, side):
    layer_axis = side // 2
    location = padded.shape[layer_axis + 1] - 1 if side % 2 == 0 else 0
    if layer_axis == 0:
        return padded[:, location, 1:-1, 1:-1]
    if layer_axis == 1:
        return padded[:, 1:-1, location, 1:-1]
    return padded[:, 1:-1, 1:-1, location]


def add_layer(field, side, layer):
    layer_axis = side // 2
    location = field.shape[layer_axis + 1] - 1 if side % 2 == 0 else 0
    if layer_axis == 0:
        return field.at[:, location].add(layer)
    if layer_axis == 1:
        return field.at[:, :, location].add(layer)
    return field.at[:, :, :, location].add(layer)


def advance(padded, rates, flux_mats):
    interior = padded[:, 1:-1, 1:-1, 1:-1]
    divergence = jnp.zeros_like(interior)
    for direction in range(3):
        if direction == 0:
            strip = padded[:, :, 1:-1, 1:-1]
        elif direction == 1:
            strip = padded[:, 1:-1, :, 1:-1]
        else:
            strip = padded[:, 1:-1, 1:-1, :]
        length = strip.shape[direction + 1]
        left_cells = lax.slice_in_dim(strip, 0, length - 1, axis=direction + 1)
        right_cells = lax.slice_in_dim(strip, 1, length, axis=direction + 1)
        average = 0.5 * (left_cells + right_cells)
        difference = right_cells - left_cells
        spread = jnp.sqrt(1.0 + average[0] * average[0])
        face_flux = (
            jnp.einsum(
                "ij,jxyz->ixyz", flux_mats[direction], average, precision=lax.Precision.HIGHEST
            )
            - 0.5 * spread * difference
        )
        count = face_flux.shape[direction + 1]
        divergence = (
            divergence
            + lax.slice_in_dim(face_flux, 1, count, axis=direction + 1)
            - lax.slice_in_dim(face_flux, 0, count - 1, axis=direction + 1)
        )
    return interior - time_step * rates * divergence - damping * jnp.tanh(interior)


def pick(pieces, sources):
    count = pieces[0].shape[0]
    positions = jnp.arange(count, dtype=jnp.int32)
    result = []
    for side in range(6):
        weight = (positions == sources[side]).astype(jnp.float32)
        piece = pieces[side // 2][:, 1 - side % 2]
        result.append(jnp.sum(weight.reshape((count, 1, 1, 1)) * piece, axis=0))
    return tuple(result)


def side_pairs(layers):
    return [jnp.stack([layers[2 * pair], layers[2 * pair + 1]])[None] for pair in range(3)]


def on_device(checkpoint, seeds, cell_rate, flux_mats, owner, neighbours, orientation):
    restored = lax.all_gather(checkpoint, "ckpt", axis=2, tiled=True)[0]
    rates = cell_rate[0]
    block_count = owner.shape[0]
    indices = jnp.arange(block_count, dtype=jnp.int32)
    position = lax.axis_index("space")
    own_block = jnp.sum(jnp.where(owner == position, indices, 0))
    chosen = (indices == own_block).astype(jnp.int32)[:, None]
    across = jnp.sum(chosen * neighbours, axis=0)
    flips = jnp.sum(chosen * orientation, axis=0)
    sources = jnp.sum(
        (indices[None, :] == across[:, None]).astype(jnp.int32) * owner[None, :], axis=1
    )

    def gather_step(pieces):
        return pick(pieces, sources)

    def fetch(field):
        layers = [boundary(field, side) for side in range(6)]
        x_faces, y_faces, z_faces = side_pairs(layers)
        whole = gather_step(
            (
                lax.all_gather(x_faces, "space", axis=0, tiled=True),
                lax.all_gather(y_faces, "space", axis=0, tiled=True),
                lax.all_gather(z_faces, "space", axis=0, tiled=True),
            )
        )
        return [reorient(whole[side], flips[side]) for side in range(6)]

    padded_states = []
    state = restored
    for section in range(STEPS):
        padded = pad_with(state, fetch(state))
        padded_states.append(padded)
        state = advance(padded, rates, flux_mats)
    adjoint_now = seeds[0, 0]
    for section in reversed(range(STEPS)):
        _, pullback = jax.vjp(lambda grid: advance(grid, rates, flux_mats), padded_states[section])
        cotangent = pullback(adjoint_now)[0]
        x_ghosts, y_ghosts, z_ghosts = side_pairs(
            [ghost_layer(cotangent, side) for side in range(6)]
        )
        incoming = gather_step(
            (
                lax.all_gather(x_ghosts, "space", axis=0, tiled=True),
                lax.all_gather(y_ghosts, "space", axis=0, tiled=True),
                lax.all_gather(z_ghosts, "space", axis=0, tiled=True),
            )
        )
        adjoint_now = cotangent[:, 1:-1, 1:-1, 1:-1]
        for side in range(6):
            adjoint_now = add_layer(adjoint_now, side, reorient(incoming[side], flips[side]))
    return (adjoint_now[None, None], state[None])


def solution(mesh):
    return jax.shard_map(
        on_device,
        mesh=mesh,
        in_specs=(
            P("space", None, "ckpt", None, None),
            P("ckpt", "space", None, None, None, None),
            P("space", None, None, None),
            P(),
            P(),
            P(),
            P(),
        ),
        out_specs=(P("ckpt", "space", None, None, None, None), P("space", None, None, None, None)),
        check_vma=False,
    )
```

profile of v0, /device:TPU:0, one launch (start us, length us, event | category | flops | bytes accessed | tf_op | source)
XLA Modules:
  0.0 1620.6 jit_solution(11246195897142510362)
XLA Ops:
  8.2 11.1 all_gather.39
  42.4 149.0 %all-gather.2 = f32[64,6,16,16]{3,2,1,0:T(8,128)S(1)} all-gather(f32[2,6,16,16]{3,2,1,0:T(8,128)S(1)} %pad_maximum_fusion.2), channel_id=4, replica_groups=mesh['ckpt'=4,'space'=32] {'space'}, dimensions={0}, use_global_device_ids=true | all-gather | bytes 405504 | tf_op jit(solution)/shard_map/all_gather | solution.py:126
  202.7 139.0 %all-gather.21.cloned.1.call-done = f32[64,6,16,128]{3,2,1,0:T(8,128)} async-done(((f32[2,6,16,128]{3,2,1,0:T(8,128)}), f32[64,6,16,128]{3,2,1,0:T(8,128)}) %all-gather.21.cloned.1.call-update) | async-done | bytes 3145744 | tf_op jit(solution)/shard_map/all_gather | solution.py:124
  348.9 2.4 scatter.40
  351.3 3.2 scatter.41
  354.6 19.7 %scatter.44 = f32[6,18,18,130]{3,2,0,1:T(8,128)S(1)} dynamic-update-slice(f32[6,18,18,130]{3,2,0,1:T(8,128)S(1)} %scatter.41, f32[6,16,1,128]{3,2,0,1:T(1,128)} %copy.1412, s32[]{:T(128)} %constant.830.clone.1, s32[]{:T(128)} %constant.831.clone.1, s32[]{:T(128)} %constant.834.clone.1, s32[]{:T(128)} %constant.831.clone.1) | dynamic-update-slice | bytes 98308 | tf_op jit(solution)/shard_map/scatter | solution.py:30
  374.2 19.7 %scatter.45 = f32[6,18,18,130]{3,2,0,1:T(8,128)S(1)} dynamic-update-slice(f32[6,18,18,130]{3,2,0,1:T(8,128)S(1)} %scatter.44, f32[6,16,1,128]{3,2,0,1:T(1,128)} %copy.1414, s32[]{:T(128)} %constant.830.clone.1, s32[]{:T(128)} %constant.831.clone.1, s32[]{:T(128)} %constant.830.clone.1, s32[]{:T(128)} %constant.831.clone.1) | dynamic-update-slice | bytes 98308 | tf_op jit(solution)/shard_map/scatter | solution.py:30
  393.9 23.4 %scatter.46 = f32[6,18,18,130]{3,2,0,1:T(8,128)S(1)} dynamic-update-slice(f32[6,18,18,130]{3,2,0,1:T(8,128)S(1)} %scatter.45, f32[6,16,16,1]{3,2,0,1:T(8,128)} %copy.1417, s32[]{:T(128)} %constant.830.clone.1, s32[]{:T(128)} %constant.831.clone.1, s32[]{:T(128)} %constant.831.clone.1, s32[]{:T(128)} %constant.835.clone.1) | dynamic-update-slice | bytes 12292 | tf_op jit(solution)/shard_map/scatter | solution.py:32
  417.4 12.1 scatter.49
  433.9 2.8 fusion.6
  444.4 3.4 pad.200
  452.7 151.3 %all-gather.5 = f32[64,6,16,16]{3,2,1,0:T(8,128)S(1)} all-gather(f32[2,6,16,16]{3,2,1,0:T(8,128)S(1)} %pad_maximum_fusion.5), channel_id=7, replica_groups=mesh['ckpt'=4,'space'=32] {'space'}, dimensions={0}, use_global_device_ids=true | all-gather | bytes 405504 | tf_op jit(solution)/shard_map/all_gather | solution.py:126
  621.3 147.7 %all-gather.25.cloned.1.call-done = f32[64,6,16,128]{3,2,1,0:T(8,128)} async-done(((f32[2,6,16,128]{3,2,1,0:T(8,128)}), f32[64,6,16,128]{3,2,1,0:T(8,128)}) %all-gather.25.cloned.1.call-update) | async-done | bytes 3145744 | tf_op jit(solution)/shard_map/all_gather | solution.py:124
  776.7 3.7 scatter.50
  780.4 3.7 scatter.51
  784.1 18.2 %scatter.54 = f32[6,18,18,130]{3,2,0,1:T(8,128)} dynamic-update-slice(f32[6,18,18,130]{3,2,0,1:T(8,128)} %scatter.51, f32[6,16,1,128]{3,2,0,1:T(1,128)} %copy.1436, s32[]{:T(128)} %constant.830.clone.1, s32[]{:T(128)} %constant.831.clone.1, s32[]{:T(128)} %constant.834.clone.1, s32[]{:T(128)} %constant.831.clone.1) | dynamic-update-slice | bytes 98308 | tf_op jit(solution)/shard_map/scatter | solution.py:30
  802.3 18.2 %scatter.55 = f32[6,18,18,130]{3,2,0,1:T(8,128)} dynamic-update-slice(f32[6,18,18,130]{3,2,0,1:T(8,128)} %scatter.54, f32[6,16,1,128]{3,2,0,1:T(1,128)} %copy.1438, s32[]{:T(128)} %constant.830.clone.1, s32[]{:T(128)} %constant.831.clone.1, s32[]{:T(128)} %constant.830.clone.1, s32[]{:T(128)} %constant.831.clone.1) | dynamic-update-slice | bytes 98308 | tf_op jit(solution)/shard_map/scatter | solution.py:30
  820.4 18.2 %scatter.56 = f32[6,18,18,130]{3,2,0,1:T(8,128)} dynamic-update-slice(f32[6,18,18,130]{3,2,0,1:T(8,128)} %scatter.55, f32[6,16,16,1]{3,2,0,1:T(8,128)} %copy.1442, s32[]{:T(128)} %constant.830.clone.1, s32[]{:T(128)} %constant.831.clone.1, s32[]{:T(128)} %constant.831.clone.1, s32[]{:T(128)} %constant.835.clone.1) | dynamic-update-slice | bytes 12292 | tf_op jit(solution)/shard_map/scatter | solution.py:32
  838.6 6.2 scatter.59
  844.8 2.9 add_multiply_fusion
  847.7 2.8 fusion
  856.0 2.8 fusion.4
  870.8 2.8 pad_add_fusion.17
  873.6 2.4 copy.1468
  876.0 2.4 copy.1469
  879.2 146.6 %all-gather.8 = f32[64,6,16,16]{3,2,1,0:T(8,128)S(1)} all-gather(f32[2,6,16,16]{3,2,1,0:T(8,128)S(1)} %pad_maximum_fusion.8), channel_id=10, replica_groups=mesh['ckpt'=4,'space'=32] {'space'}, dimensions={0}, use_global_device_ids=true | all-gather | bytes 405504 | tf_op jit(solution)/shard_map/all_gather | solution.py:148
  1040.7 2.3 copy.1471
  1043.0 4.0 pad_add_fusion.3
  1048.3 2.8 fusion.27
  1062.6 132.1 %all-gather.29.cloned.1.call-done = f32[64,6,16,128]{3,2,1,0:T(8,128)} async-done(((f32[2,6,16,128]{3,2,1,0:T(8,128)}), f32[64,6,16,128]{3,2,1,0:T(8,128)}) %all-gather.29.cloned.1.call-update) | async-done | bytes 3145744 | tf_op jit(solution)/shard_map/all_gather | solution.py:146
  1194.7 2.8 fusion.31
  1210.3 2.7 scatter-add.44
  1214.1 2.7 scatter-add.45
  1216.8 2.6 slice_add_fusion.5
  1219.4 9.4 scatter-add.46
  1231.0 3.8 scatter-add.49
  1243.4 2.8 fusion.2
  1256.0 142.5 %all-gather.11 = f32[64,6,16,16]{3,2,1,0:T(8,128)S(1)} all-gather(f32[2,6,16,16]{3,2,1,0:T(8,128)S(1)} %pad_maximum_fusion.11), channel_id=13, replica_groups=mesh['ckpt'=4,'space'=32] {'space'}, dimensions={0}, use_global_device_ids=true | all-gather | bytes 405504 | tf_op jit(solution)/shard_map/all_gather | solution.py:148
  1405.2 2.4 copy.1509
  1413.4 2.3 copy.1507
  1415.7 3.3 pad_add_fusion
  1420.3 2.8 fusion.15
  1434.6 134.8 %all-gather.33.cloned.1.call-done = f32[64,6,16,128]{3,2,1,0:T(8,128)} async-done(((f32[2,6,16,128]{3,2,1,0:T(8,128)}), f32[64,6,16,128]{3,2,1,0:T(8,128)}) %all-gather.33.cloned.1.call-update) | async-done | bytes 3145744 | tf_op jit(solution)/shard_map/all_gather | solution.py:146
  1569.4 2.8 fusion.19
  1585.0 2.7 scatter-add.54
  1588.7 2.7 scatter-add.55
  1593.2 12.2 scatter-add.56
  1606.8 5.8 scatter-add.59
  (354 shorter events, 191.6 us)
Async XLA Ops:
  7.2 13.7 copy-start.55
  7.2 15.0 copy-start.54
  7.2 15.0 copy-start.53
  7.2 191.8 %all-gather.23.cloned.1.call-start = ((), (), s32[]{:S(2)}) async-start(), calls=%async_computation.1 | async-start | bytes 3244032 | tf_op jit(solution)/shard_map/all_gather | solution.py:125
  20.1 321.7 %all-gather.21.cloned.1.call-start = ((), (), s32[]{:S(2)}) async-start(), calls=%async_computation | async-start | bytes 3244032 | tf_op jit(solution)/shard_map/all_gather | solution.py:124
  20.8 592.2 %all-gather.27.cloned.1.call-start = ((), (), s32[]{:S(2)}) async-start(), calls=%async_computation.3 | async-start | bytes 3244032 | tf_op jit(solution)/shard_map/all_gather | solution.py:125
  41.7 149.7 %copy-start.41 = (f32[32]{0:T(128)}, f32[32]{0:T(128)S(1)}, u32[]{:S(2)}) copy-start(f32[32]{0:T(128)S(1)} %compare_convert_fusion) | copy-start | bytes 388
  42.4 149.0 %copy-start.45 = (f32[32]{0:T(128)}, f32[32]{0:T(128)S(1)}, u32[]{:S(2)}) copy-start(f32[32]{0:T(128)S(1)} %compare_convert_fusion.1) | copy-start | bytes 388
  195.0 3.3 copy-start.38
  196.4 145.3 %copy-start.49 = (f32[32]{0:T(128)}, f32[32]{0:T(128)S(1)}, u32[]{:S(2)}) copy-start(f32[32]{0:T(128)S(1)} %compare_convert_fusion.4) | copy-start | bytes 388
  197.1 144.6 %copy-start.51 = (f32[32]{0:T(128)}, f32[32]{0:T(128)S(1)}, u32[]{:S(2)}) copy-start(f32[32]{0:T(128)S(1)} %compare_convert_fusion.5) | copy-start | bytes 388
  198.3 2.9 copy-start.39
  343.9 73.4 %copy-start.15 = (f32[6,16,16,1]{3,2,0,1:T(8,128)S(1)}, f32[6,16,16,1]{3,2,0,1:T(8,128)}, u32[]{:S(2)}) copy-start(f32[6,16,16,1]{3,2,0,1:T(8,128)} %copy.1418) | copy-start | bytes 18436
  430.7 2.7 copy-start.11
  430.9 5.9 copy-start.24
  433.4 3.9 copy-start.22
  433.9 2.8 copy-start.10
  436.8 1.3 copy-start.13
  442.5 326.5 %all-gather.25.cloned.1.call-start = ((), (), s32[]{:S(2)}) async-start(), calls=%async_computation.2 | async-start | bytes 3244032 | tf_op jit(solution)/shard_map/all_gather | solution.py:124
  444.1 604.2 %all-gather.31.cloned.1.call-start = ((), (), s32[]{:S(2)}) async-start(), calls=%async_computation.5 | async-start | bytes 3244032 | tf_op jit(solution)/shard_map/all_gather | solution.py:147
  444.3 3.4 copy-start.8
  452.7 151.3 %copy-start.42 = (f32[32]{0:T(128)S(1)}, f32[32]{0:T(128)}, u32[]{:S(2)}) copy-start(f32[32]{0:T(128)} %copy-done.41) | copy-start | bytes 388
  452.7 151.3 %copy-start.46 = (f32[32]{0:T(128)S(1)}, f32[32]{0:T(128)}, u32[]{:S(2)}) copy-start(f32[32]{0:T(128)} %copy-done.45) | copy-start | bytes 388
  847.7 2.9 copy-start
  853.0 1.4 copy-start.6
  864.8 3.7 copy-start.1
  865.3 3.1 copy-start.2
  870.0 324.6 %all-gather.29.cloned.1.call-start = ((), (), s32[]{:S(2)}) async-start(), calls=%async_computation.4 | async-start | bytes 3244032 | tf_op jit(solution)/shard_map/all_gather | solution.py:146
  870.8 549.5 %all-gather.35.cloned.1.call-start = ((), (), s32[]{:S(2)}) async-start(), calls=%async_computation.7 | async-start | bytes 3244032 | tf_op jit(solution)/shard_map/all_gather | solution.py:147
  879.2 146.6 %copy-start.43 = (f32[32]{0:T(128)S(1)}, f32[32]{0:T(128)}, u32[]{:S(2)}) copy-start(f32[32]{0:T(128)} %copy-done.41) | copy-start | bytes 388
  879.2 146.6 %copy-start.47 = (f32[32]{0:T(128)S(1)}, f32[32]{0:T(128)}, u32[]{:S(2)}) copy-start(f32[32]{0:T(128)} %copy-done.45) | copy-start | bytes 388
  1206.1 1.7 copy-start.27
  1206.1 1.7 copy-start.35
  1206.1 3.1 copy-start.37
  1216.8 12.0 copy-start.17
  1243.3 3.8 copy-start.25
  1248.4 2.3 copy-start.3
  1251.5 317.9 %all-gather.33.cloned.1.call-start = ((), (), s32[]{:S(2)}) async-start(), calls=%async_computation.6 | async-start | bytes 3244032 | tf_op jit(solution)/shard_map/all_gather | solution.py:146
  1253.1 2.2 copy-start.4
  1256.0 142.5 %copy-start.44 = (f32[32]{0:T(128)S(1)}, f32[32]{0:T(128)}, u32[]{:S(2)}) copy-start(f32[32]{0:T(128)} %copy-done.41) | copy-start | bytes 388
  1256.0 142.5 %copy-start.48 = (f32[32]{0:T(128)S(1)}, f32[32]{0:T(128)}, u32[]{:S(2)}) copy-start(f32[32]{0:T(128)} %copy-done.45) | copy-start | bytes 388
  1420.3 149.2 %copy-start.50 = (f32[32]{0:T(128)S(1)}, f32[32]{0:T(128)}, u32[]{:S(2)}) copy-start(f32[32]{0:T(128)} %copy-done.49) | copy-start | bytes 388
  1420.3 149.2 %copy-start.52 = (f32[32]{0:T(128)S(1)}, f32[32]{0:T(128)}, u32[]{:S(2)}) copy-start(f32[32]{0:T(128)} %copy-done.51) | copy-start | bytes 388
  1580.9 1.6 copy-start.26
  1580.9 1.6 copy-start.34
  1580.9 3.0 copy-start.36
  1591.4 1.8 copy-start.9
  1591.4 14.0 copy-start.16
  (16 other events, 14.8 us)
Sparse Core Ops, SparseCore 0:
  20.2 163.9 all-gather.22
  185.8 155.8 all-gather.20
  442.6 169.6 all-gather.26
  613.8 155.1 all-gather.24
  870.1 164.8 all-gather.30
  1036.5 158.0 all-gather.28
  1251.6 165.3 all-gather.34
  1418.7 150.6 all-gather.32
where the time goes:
time: 1630 us; the launch traced here: 1620 us
  blocking collectives  600 us (37%)
  waiting for transfers between devices  554 us (34%)
  local copies, waits for them, and re-layouts  287 us (18%)
  other arithmetic  127 us (8%)
  between operations  31.1 us (2%)
  matrix products  21 us (1%)
    all_gather x2, blocking collectives, fetch(): lax.all_gather(z_faces, 'space', axis=0, tiled=True)  300 us
    all_gather x2, blocking collectives, on_device(): lax.all_gather(z_ghosts, 'space', axis=0, tiled=True)  289 us
    all_gather x2, waiting for transfers between devices, fetch(): lax.all_gather(x_faces, 'space', axis=0, tiled=True)  287 us
    all_gather x2, waiting for transfers between devices, on_device(): lax.all_gather(x_ghosts, 'space', axis=0, tiled=True)  267 us
    scatter x4, local copies, waits for them, and re-layouts, pad_with(): padded = padded.at[:, 1:-1, location, 1:-1].set(ghosts[side])  75.7 us
    scatter x4, local copies, waits for them, and re-layouts, pad_with(): padded = padded.at[:, 1:-1, 1:-1, location].set(ghosts[side])  59.9 us
  transfers between devices with their start and end apart: 8, of which 4 were waited for; matrix products, arithmetic and copies ran while one was open for 8% of the time, Pallas kernels for 0%

commit v1 on v0

--- a/solution.py
+++ b/solution.py
@@ -119,9 +119,18 @@
     def fetch(field):
         layers = [boundary(field, side) for side in range(6)]
         x_faces, y_faces, z_faces = side_pairs(layers)
+        find_racks = lambda x_local, lane_axis, where_dim: jnp.concatenate(
+            lax.all_to_all(
+                jnp.stack([x_local for _ in range(lax.axis_size(lane_axis))]),
+                axis_name=lane_axis,
+                split_axis=0,
+                concat_axis=0,
+            ),
+            axis=where_dim,
+        )
         whole = gather_step(
             (
-                lax.all_gather(x_faces, "space", axis=0, tiled=True),
+                find_racks(x_faces, "space", 0),
                 lax.all_gather(y_faces, "space", axis=0, tiled=True),
                 lax.all_gather(z_faces, "space", axis=0, tiled=True),
             )

time: 1630 us -> 1430 us (0.88)
  waiting for transfers between devices: 554 us -> 263 us
  blocking collectives: 600 us -> 670 us
  starting transfers between devices: 0.55 us -> 24.4 us
    all_gather x2 -> x0, waiting for transfers between devices: 287 us -> none  [fetch(): lax.all_gather(x_faces, 'space', axis=0, tiled=True)]
    all_gather x2, blocking collectives: 300 us -> 356 us  [fetch(): lax.all_gather(z_faces, 'space', axis=0, tiled=True)]
    all_to_all x0 -> x2, starting transfers between devices: none -> 24 us  [fetch(): lax.all_to_all(jnp.stack([x_local for _ in range(lax.axis_size(lane_axis)...]
  transfers between devices with their start and end apart: 8 -> 8, of which waited for: 4 -> 2; matrix products, arithmetic and copies ran while one was open for 8% -> 10% of each run, Pallas kernels for 0% -> 0%
where the time goes in v1:
time: 1430 us; the launch traced here: 1420 us
  blocking collectives  670 us (47%)
  local copies, waits for them, and re-layouts  294 us (21%)
  waiting for transfers between devices  263 us (18%)
  other arithmetic  121 us (8%)
  between operations  31.1 us (2%)
  starting transfers between devices  24.4 us (2%)
  matrix products  21 us (1%)
    all_gather x2, blocking collectives, fetch(): lax.all_gather(z_faces, 'space', axis=0, tiled=True)  356 us
    all_gather x2, blocking collectives, on_device(): lax.all_gather(z_ghosts, 'space', axis=0, tiled=True)  303 us
    all_gather x2, waiting for transfers between devices, on_device(): lax.all_gather(x_ghosts, 'space', axis=0, tiled=True)  263 us
    scatter x4, local copies, waits for them, and re-layouts, pad_with(): padded = padded.at[:, 1:-1, location, 1:-1].set(ghosts[side])  76.3 us
    scatter x4, local copies, waits for them, and re-layouts, pad_with(): padded = padded.at[:, 1:-1, 1:-1, location].set(ghosts[side])  59.8 us
    scatter-add x4, local copies, waits for them, and re-layouts, add_layer(): return field.at[:, :, :, location].add(layer)  31.2 us
  transfers between devices with their start and end apart: 8, of which 2 were waited for; matrix products, arithmetic and copies ran while one was open for 10% of the time, Pallas kernels for 0%

profile of v1, /device:TPU:0, one launch (start us, length us, event | category | flops | bytes accessed | tf_op | source)
XLA Modules:
  0.0 1424.3 jit_solution(16430721316513946912)
XLA Ops:
  8.2 11.1 all_gather.33
  22.1 8.0 all-to-all-start
  51.6 175.5 %all-gather.1 = f32[64,6,16,16]{3,2,1,0:T(8,128)S(1)} all-gather(f32[2,6,16,16]{3,2,1,0:T(8,128)S(1)} %pad_maximum_fusion.2), channel_id=3, replica_groups=mesh['ckpt'=4,'space'=32] {'space'}, dimensions={0}, use_global_device_ids=true | all-gather | bytes 405504 | tf_op jit(solution)/shard_map/all_gather | solution.py:135
  237.3 2.4 scatter.40
  239.8 2.4 scatter.41
  248.7 19.9 %scatter.44 = f32[6,18,18,130]{3,2,0,1:T(8,128)S(1)} dynamic-update-slice(f32[6,18,18,130]{3,2,0,1:T(8,128)S(1)} %scatter.41, f32[6,16,1,128]{3,2,0,1:T(1,128)S(1)} %copy.1445, s32[]{:T(128)} %constant.830.clone.1, s32[]{:T(128)} %constant.831.clone.1, s32[]{:T(128)} %constant.834.clone.1, s32[]{:T(128)} %constant.831.clone.1) | dynamic-update-slice | bytes 98308 | tf_op jit(solution)/shard_map/scatter | solution.py:30
  268.6 19.7 %scatter.45 = f32[6,18,18,130]{3,2,0,1:T(8,128)S(1)} dynamic-update-slice(f32[6,18,18,130]{3,2,0,1:T(8,128)S(1)} %scatter.44, f32[6,16,1,128]{3,2,0,1:T(1,128)} %copy.1447, s32[]{:T(128)} %constant.830.clone.1, s32[]{:T(128)} %constant.831.clone.1, s32[]{:T(128)} %constant.830.clone.1, s32[]{:T(128)} %constant.831.clone.1) | dynamic-update-slice | bytes 98308 | tf_op jit(solution)/shard_map/scatter | solution.py:30
  288.3 23.4 %scatter.46 = f32[6,18,18,130]{3,2,0,1:T(8,128)S(1)} dynamic-update-slice(f32[6,18,18,130]{3,2,0,1:T(8,128)S(1)} %scatter.45, f32[6,16,16,1]{3,2,0,1:T(8,128)} %copy.1450, s32[]{:T(128)} %constant.830.clone.1, s32[]{:T(128)} %constant.831.clone.1, s32[]{:T(128)} %constant.831.clone.1, s32[]{:T(128)} %constant.835.clone.1) | dynamic-update-slice | bytes 12292 | tf_op jit(solution)/shard_map/scatter | solution.py:32
  311.7 12.1 scatter.49
  328.3 2.8 fusion.6
  339.8 16.0 %all-to-all-start.1 = ((f32[32,1,2,6,16,128]{5,4,3,2,1,0:T(8,128)}), f32[32,1,2,6,16,128]{5,4,3,2,1,0:T(8,128)}, u32[]{:S(2)}, u32[]{:S(2)}) async-start(f32[32,1,2,6,16,128]{5,4,3,2,1,0:T(8,128)} %stack.47), calls=%async_computation.1 | async-start | bytes 6291456 | tf_op jit(solution)/shard_map/all_to_all | solution.py:123
  356.0 3.4 pad.200
  364.3 180.4 %all-gather.3 = f32[64,6,16,16]{3,2,1,0:T(8,128)S(1)} all-gather(f32[2,6,16,16]{3,2,1,0:T(8,128)S(1)} %pad_maximum_fusion.5), channel_id=5, replica_groups=mesh['ckpt'=4,'space'=32] {'space'}, dimensions={0}, use_global_device_ids=true | all-gather | bytes 405504 | tf_op jit(solution)/shard_map/all_gather | solution.py:135
  548.5 2.3 copy.1476
  561.7 3.7 scatter.50
  566.2 3.7 scatter.51
  577.7 18.6 %scatter.54 = f32[6,18,18,130]{3,2,0,1:T(8,128)} dynamic-update-slice(f32[6,18,18,130]{3,2,0,1:T(8,128)} %scatter.51, f32[6,16,1,128]{3,2,0,1:T(1,128)S(1)} %copy.1468, s32[]{:T(128)} %constant.830.clone.1, s32[]{:T(128)} %constant.831.clone.1, s32[]{:T(128)} %constant.834.clone.1, s32[]{:T(128)} %constant.831.clone.1) | dynamic-update-slice | bytes 98308 | tf_op jit(solution)/shard_map/scatter | solution.py:30
  596.3 18.1 %scatter.55 = f32[6,18,18,130]{3,2,0,1:T(8,128)} dynamic-update-slice(f32[6,18,18,130]{3,2,0,1:T(8,128)} %scatter.54, f32[6,16,1,128]{3,2,0,1:T(1,128)} %copy.1470, s32[]{:T(128)} %constant.830.clone.1, s32[]{:T(128)} %constant.831.clone.1, s32[]{:T(128)} %constant.830.clone.1, s32[]{:T(128)} %constant.831.clone.1) | dynamic-update-slice | bytes 98308 | tf_op jit(solution)/shard_map/scatter | solution.py:30
  614.5 18.2 %scatter.56 = f32[6,18,18,130]{3,2,0,1:T(8,128)} dynamic-update-slice(f32[6,18,18,130]{3,2,0,1:T(8,128)} %scatter.55, f32[6,16,16,1]{3,2,0,1:T(8,128)} %copy.1474, s32[]{:T(128)} %constant.830.clone.1, s32[]{:T(128)} %constant.831.clone.1, s32[]{:T(128)} %constant.831.clone.1, s32[]{:T(128)} %constant.835.clone.1) | dynamic-update-slice | bytes 12292 | tf_op jit(solution)/shard_map/scatter | solution.py:32
  632.7 6.1 scatter.59
  638.8 2.9 add_multiply_fusion
  641.7 2.8 fusion
  650.0 2.8 fusion.4
  664.8 2.8 pad_add_fusion.17
  667.6 2.4 copy.1499
  670.0 2.4 copy.1500
  673.2 154.9 %all-gather.6 = f32[64,6,16,16]{3,2,1,0:T(8,128)S(1)} all-gather(f32[2,6,16,16]{3,2,1,0:T(8,128)S(1)} %pad_maximum_fusion.8), channel_id=8, replica_groups=mesh['ckpt'=4,'space'=32] {'space'}, dimensions={0}, use_global_device_ids=true | all-gather | bytes 405504 | tf_op jit(solution)/shard_map/all_gather | solution.py:157
  842.9 2.3 copy.1502
  845.2 4.0 pad_add_fusion.3
  850.4 2.8 fusion.27
  864.7 129.9 %all-gather.21.cloned.1.call-done = f32[64,6,16,128]{3,2,1,0:T(8,128)} async-done(((f32[2,6,16,128]{3,2,1,0:T(8,128)}), f32[64,6,16,128]{3,2,1,0:T(8,128)}) %all-gather.21.cloned.1.call-update) | async-done | bytes 3145744 | tf_op jit(solution)/shard_map/all_gather | solution.py:155
  994.7 2.8 fusion.31
  1010.3 2.7 scatter-add.44
  1014.1 2.7 scatter-add.45
  1016.8 2.6 slice_add_fusion.5
  1019.4 9.4 scatter-add.46
  1031.0 3.8 scatter-add.49
  1043.4 2.8 fusion.2
  1056.0 148.1 %all-gather.9 = f32[64,6,16,16]{3,2,1,0:T(8,128)S(1)} all-gather(f32[2,6,16,16]{3,2,1,0:T(8,128)S(1)} %pad_maximum_fusion.11), channel_id=11, replica_groups=mesh['ckpt'=4,'space'=32] {'space'}, dimensions={0}, use_global_device_ids=true | all-gather | bytes 405504 | tf_op jit(solution)/shard_map/all_gather | solution.py:157
  1218.9 2.4 copy.1538
  1221.3 3.3 pad_add_fusion
  1225.9 2.8 fusion.15
  1240.3 132.8 %all-gather.25.cloned.1.call-done = f32[64,6,16,128]{3,2,1,0:T(8,128)} async-done(((f32[2,6,16,128]{3,2,1,0:T(8,128)}), f32[64,6,16,128]{3,2,1,0:T(8,128)}) %all-gather.25.cloned.1.call-update) | async-done | bytes 3145744 | tf_op jit(solution)/shard_map/all_gather | solution.py:155
  1373.1 2.8 fusion.19
  1388.6 2.7 scatter-add.54
  1392.4 2.7 scatter-add.55
  1396.9 12.2 scatter-add.56
  1410.5 5.8 scatter-add.59
  (360 shorter events, 193.0 us)
Async XLA Ops:
  7.2 235.1 %all-gather.17.cloned.1.call-start = ((), (), s32[]{:S(2)}) async-start(), calls=%async_computation.2 | async-start | bytes 3244032 | tf_op jit(solution)/shard_map/all_gather | solution.py:134
  22.1 8.1 copy-start.57
  22.1 9.4 copy-start.55
  22.1 9.4 copy-start.56
  22.1 212.5 %all-to-all-start = ((f32[32,1,2,6,16,128]{5,4,3,2,1,0:T(8,128)}), f32[32,1,2,6,16,128]{5,4,3,2,1,0:T(8,128)}, u32[]{:S(2)}, u32[]{:S(2)}) async-start(f32[32,1,2,6,16,128]{5,4,3,2,1,0:T(8,128)} %stack.43), calls=%async_computation | async-start | bytes 6291456 | tf_op jit(solution)/shard_map/all_to_all | solution.py:123
  30.1 539.8 %all-gather.19.cloned.1.call-start = ((), (), s32[]{:S(2)}) async-start(), calls=%async_computation.3 | async-start | bytes 3244032 | tf_op jit(solution)/shard_map/all_gather | solution.py:134
  50.9 176.2 %copy-start.41 = (f32[32]{0:T(128)}, f32[32]{0:T(128)S(1)}, u32[]{:S(2)}) copy-start(f32[32]{0:T(128)S(1)} %compare_convert_fusion) | copy-start | bytes 388
  51.5 175.5 %copy-start.45 = (f32[32]{0:T(128)}, f32[32]{0:T(128)S(1)}, u32[]{:S(2)}) copy-start(f32[32]{0:T(128)S(1)} %compare_convert_fusion.1) | copy-start | bytes 388
  230.7 3.3 copy-start.38
  232.0 4.8 copy-start.49
  232.7 4.1 copy-start.52
  233.9 8.3 copy-start.39
  244.4 67.2 %copy-start.15 = (f32[6,16,16,1]{3,2,0,1:T(8,128)S(1)}, f32[6,16,16,1]{3,2,0,1:T(8,128)}, u32[]{:S(2)}) copy-start(f32[6,16,16,1]{3,2,0,1:T(8,128)} %copy.1451) | copy-start | bytes 18436
  325.0 2.7 copy-start.11
  325.2 5.9 copy-start.24
  327.8 3.9 copy-start.22
  328.2 2.8 copy-start.10
  339.8 214.0 %all-to-all-start.1 = ((f32[32,1,2,6,16,128]{5,4,3,2,1,0:T(8,128)}), f32[32,1,2,6,16,128]{5,4,3,2,1,0:T(8,128)}, u32[]{:S(2)}, u32[]{:S(2)}) async-start(f32[32,1,2,6,16,128]{5,4,3,2,1,0:T(8,128)} %stack.47), calls=%async_computation.1 | async-start | bytes 6291456 | tf_op jit(solution)/shard_map/all_to_all | solution.py:123
  355.7 494.7 %all-gather.23.cloned.1.call-start = ((), (), s32[]{:S(2)}) async-start(), calls=%async_computation.5 | async-start | bytes 3244032 | tf_op jit(solution)/shard_map/all_gather | solution.py:156
  356.0 3.4 copy-start.8
  364.3 180.4 %copy-start.42 = (f32[32]{0:T(128)S(1)}, f32[32]{0:T(128)}, u32[]{:S(2)}) copy-start(f32[32]{0:T(128)} %copy-done.41) | copy-start | bytes 388
  364.3 180.4 %copy-start.46 = (f32[32]{0:T(128)S(1)}, f32[32]{0:T(128)}, u32[]{:S(2)}) copy-start(f32[32]{0:T(128)} %copy-done.45) | copy-start | bytes 388
  553.7 2.2 copy-start.50
  553.7 2.2 copy-start.53
  556.2 2.8 copy-start.28
  641.7 2.9 copy-start
  658.8 3.7 copy-start.1
  659.3 3.1 copy-start.2
  664.0 330.7 %all-gather.21.cloned.1.call-start = ((), (), s32[]{:S(2)}) async-start(), calls=%async_computation.4 | async-start | bytes 3244032 | tf_op jit(solution)/shard_map/all_gather | solution.py:155
  664.8 561.1 %all-gather.27.cloned.1.call-start = ((), (), s32[]{:S(2)}) async-start(), calls=%async_computation.7 | async-start | bytes 3244032 | tf_op jit(solution)/shard_map/all_gather | solution.py:156
  673.2 154.9 %copy-start.43 = (f32[32]{0:T(128)S(1)}, f32[32]{0:T(128)}, u32[]{:S(2)}) copy-start(f32[32]{0:T(128)} %copy-done.41) | copy-start | bytes 388
  673.2 154.9 %copy-start.47 = (f32[32]{0:T(128)S(1)}, f32[32]{0:T(128)}, u32[]{:S(2)}) copy-start(f32[32]{0:T(128)} %copy-done.45) | copy-start | bytes 388
  1006.1 1.7 copy-start.27
  1006.1 1.7 copy-start.35
  1006.2 3.1 copy-start.37
  1016.8 12.0 copy-start.17
  1043.3 3.8 copy-start.25
  1048.4 2.3 copy-start.3
  1051.5 321.5 %all-gather.25.cloned.1.call-start = ((), (), s32[]{:S(2)}) async-start(), calls=%async_computation.6 | async-start | bytes 3244032 | tf_op jit(solution)/shard_map/all_gather | solution.py:155
  1053.1 2.2 copy-start.4
  1056.0 148.1 %copy-start.44 = (f32[32]{0:T(128)S(1)}, f32[32]{0:T(128)}, u32[]{:S(2)}) copy-start(f32[32]{0:T(128)} %copy-done.41) | copy-start | bytes 388
  1056.0 148.1 %copy-start.48 = (f32[32]{0:T(128)S(1)}, f32[32]{0:T(128)}, u32[]{:S(2)}) copy-start(f32[32]{0:T(128)} %copy-done.45) | copy-start | bytes 388
  1225.9 147.2 %copy-start.51 = (f32[32]{0:T(128)S(1)}, f32[32]{0:T(128)}, u32[]{:S(2)}) copy-start(f32[32]{0:T(128)} %copy-done.49) | copy-start | bytes 388
  1225.9 147.2 %copy-start.54 = (f32[32]{0:T(128)S(1)}, f32[32]{0:T(128)}, u32[]{:S(2)}) copy-start(f32[32]{0:T(128)} %copy-done.52) | copy-start | bytes 388
  1384.6 1.6 copy-start.34
  1384.6 3.0 copy-start.36
  1395.1 1.8 copy-start.9
  1395.1 14.0 copy-start.16
  (18 other events, 18.3 us)
Sparse Core Ops, SparseCore 0:
  20.1 209.1 all-gather.16
  337.0 204.4 all-gather.18
  664.1 169.3 all-gather.22
  835.0 159.6 all-gather.20
  1051.6 165.5 all-gather.26
  1218.7 154.3 all-gather.24
